TPU v7x, 128 devices: a whole 4x4x4 slice. The times are simulated.
128 devices in a mesh: fsdp: 16 (over x_hi, y, core), loop: 8 (over z, x_lo).
Axes of the slice: x: 4 (x_hi: 2, x_lo: 2; x = x_hi * 2 + x_lo), y: 4, z: 4, core: 2. Of those that a mesh axis runs over, the one named last changes fastest.
Arguments:
- iterate: bfloat16 [8, 7168, 2048], P(None, 'fsdp', 'loop'), may hold values from -0.0625 to 0.0625
- expert_order: int32 [8], replicated, may hold values from 0 to 7, each once
Outputs:
- update: bfloat16 [8, 7168, 2048], P(None, 'fsdp', 'loop')
Inputs may be any that keep to these rules, and one draw needn't show every extreme that they name: `expert_order`: each value names a different expert.
All inputs are finite; a program needn't handle non-finite values.
Results may differ from a plain program's by a relative error of at most 0.006.
Values may be sent and summed in bfloat16 or wider, within the bound.
A program may use at most 128 MiB of HBM per device.

v0:
```python
import jax
import jax.numpy as jnp
from jax import lax
from jax.sharding import PartitionSpec as P

D = 7168
coef_linear = 3.4445
coef_cubic = -4.775


def half_step(left, right):
    factor = 0.2 * D**0.5
    partial_gram = jnp.einsum("eic,eik->eck", left, right, preferred_element_type=jnp.float32)
    summed = lax.psum(partial_gram, "fsdp")
    gram_block = summed.astype(jnp.bfloat16)
    product = jnp.einsum("eik,eck->eic", right, gram_block, preferred_element_type=jnp.float32)
    result = factor * (coef_linear * left.astype(jnp.float32) + coef_cubic * product)
    return result.astype(jnp.bfloat16)


def body(iterate, expert_order):
    chosen = jnp.take(iterate, expert_order, axis=0)
    gathered = lax.all_gather(chosen, "loop", axis=2, tiled=True)
    return half_step(chosen, gathered)


def solution(mesh):
    placed = (P(None, "fsdp", "loop"), P())
    return jax.shard_map(
        body, mesh=mesh, in_specs=placed, out_specs=P(None, "fsdp", "loop"), check_vma=False
    )
```

profile of v0, /device:TPU:6, one launch (start us, length us, event | category | flops | bytes accessed | tf_op | source)
XLA Modules:
  0.0 530.2 jit_solution(17105883795488496706)
XLA Ops:
  6.5 0.0 copy-start
  6.5 0.0 all-gather.2.cloned.1.call-start
  6.5 0.8 compare_and_fusion
  7.3 0.7 compare_select_fusion
  8.0 0.0 copy-done
  8.1 1.9 gather_fusion
  9.9 3.0 broadcast_select_fusion
  12.9 0.0 all-gather.2.cloned.1.call-update
  12.9 288.9 %all-gather.2.cloned.1.call-done = bf16[8,448,2048]{2,1,0:T(8,128)(2,1)} async-done(((bf16[8,448,256]{2,1,0:T(8,128)(2,1)}), bf16[8,448,2048]{2,1,0:T(8,128)(2,1)}) %all-gather.2.cloned.1.call-update) | async-done | bytes 14680080 | tf_op jit(solution)/shard_map/all_gather | solution.py:23
  301.8 16.0 %fusion.4 = f32[8,256,2048]{2,1,0:T(8,128)} fusion(bf16[8,448,256]{2,1,0:T(8,128)(2,1)} %broadcast_select_fusion, bf16[8,448,2048]{2,1,0:T(8,128)(2,1)} %all-gather.2.cloned.1.call-done), kind=kOutput, calls=%fused_computation.8 | convolution fusion | flops 3758096384 | bytes 33292288 | tf_op jit(solution)/shard_map/eic,eik->eck/dot_general | solution.py:13
  317.8 193.1 %all-reduce.1 = bf16[8,256,2048]{2,1,0:T(8,128)(2,1)} all-reduce(f32[8,256,2048]{2,1,0:T(8,128)} %fusion.4), channel_id=1, replica_groups=mesh['fsdp'=16,'loop'=8] {'fsdp'}, use_global_device_ids=true, to_apply=%region_0.1 | all-reduce | flops 4194304 | bytes 25165824 | tf_op jit(solution)/shard_map/psum | solution.py:14
  510.9 12.5 %multiply_convert_fusion = bf16[8,448,256]{2,1,0:T(8,128)(2,1)} fusion(bf16[8,448,256]{2,1,0:T(8,128)(2,1)} %broadcast_select_fusion, bf16[8,448,2048]{2,1,0:T(8,128)(2,1)} %all-gather.2.cloned.1.call-done, bf16[8,256,2048]{2,1,0:T(8,128)(2,1)} %all-reduce.1), kind=kOutput, calls=%fused_computation.3 | convolution fusion | flops 3763601408 | bytes 26738688 | tf_op jit(solution)/shard_map/eik,eck->eic/dot_general | solution.py:16
  (1 shorter events, 0.0 us)
Async XLA Ops:
  6.5 1.5 copy-start
  6.5 295.3 %all-gather.2.cloned.1.call-start = ((), (), s32[]{:S(2)}) async-start(), calls=%async_computation | async-start | bytes 16515072 | tf_op jit(solution)/shard_map/all_gather | solution.py:23
Sparse Core Ops, SparseCore 0:
  13.1 288.6 all-gather.1
where the time goes:
time: 530 us
  waiting for transfers between devices  289 us (55%)
  blocking collectives  193 us (36%)
  matrix products  28.5 us (5%)
  between operations  13.4 us (3%)
    all_gather x1, waiting for transfers between devices, body(): gathered = lax.all_gather(chosen, 'loop', axis=2, tiled=True)  289 us
    psum x1, blocking collectives, half_step(): summed = lax.psum(partial_gram, 'fsdp')  193 us
    dot_general x1, matrix products, half_step(): jnp.einsum('eic,eik->eck', left, right, preferred_element_type=jnp.float32)  16 us
    dot_general x1, matrix products, half_step(): jnp.einsum('eik,eck->eic', right, gram_block, preferred_element_type=jnp....  12.5 us
  transfers between devices with their start and end apart: 1, of which 1 were waited for; matrix products, arithmetic and copies ran while one was open for 0% of the time, Pallas kernels for 0%

commit v1 on v0

--- a/solution.py
+++ b/solution.py
@@ -1,3 +1,4 @@
+import functools
 import jax
 import jax.numpy as jnp
 from jax import lax
@@ -6,6 +7,16 @@
 D = 7168
 coef_linear = 3.4445
 coef_cubic = -4.775
+
+
+def lay_desk(state, axis_id, out_dim):
+    wide_out = jnp.stack([state for _ in range(lax.axis_size(axis_id))], axis=0)
+    return jnp.concatenate(
+        lax.all_to_all(wide_out, split_axis=0, concat_axis=0, axis_name=axis_id), axis=out_dim
+    )
+
+
+list_blocks_for = functools.partial(lay_desk, axis_id="loop", out_dim=2)
 
 
 def half_step(left, right):
@@ -20,7 +31,7 @@
 
 def body(iterate, expert_order):
     chosen = jnp.take(iterate, expert_order, axis=0)
-    gathered = lax.all_gather(chosen, "loop", axis=2, tiled=True)
+    gathered = list_blocks_for(chosen)
     return half_step(chosen, gathered)
 
 

time: 530 us -> 403 us (0.76)
  waiting for transfers between devices: 289 us -> 0 us
  blocking collectives: 193 us -> 362 us
  between operations: 13.4 us -> 0.03 us
  local copies, waits for them, and re-layouts: 1.94 us -> 10.5 us
    all_gather x1 -> x0, waiting for transfers between devices: 289 us -> none  [body(): gathered = lax.all_gather(chosen, 'loop', axis=2, tiled=True)]
    all_to_all x0 -> x1, blocking collectives: none -> 169 us  [lay_desk(): lax.all_to_all(wide_out, split_axis=0, concat_axis=0, axis_name=axis_id)]
    reshape x0 -> x1, local copies, waits for them, and re-layouts: none -> 6.72 us  [lay_desk(): jnp.concatenate(lax.all_to_all(wide_out, split_axis=0, concat_axis=0, axi...]
  transfers between devices with their start and end apart: 1 -> 0, of which waited for: 1 -> 0; matrix products, arithmetic and copies ran while one was open for 0% -> 0% of each run, Pallas kernels for 0% -> 0%
where the time goes in v1:
time: 403 us; the launch traced here: 402 us
  blocking collectives  362 us (90%)
  matrix products  25.8 us (6%)
  local copies, waits for them, and re-layouts  10.5 us (3%)
    psum x1, blocking collectives, half_step(): summed = lax.psum(partial_gram, 'fsdp')  193 us
    all_to_all x1, blocking collectives, lay_desk(): lax.all_to_all(wide_out, split_axis=0, concat_axis=0, axis_name=axis_id)  169 us
    dot_general x1, matrix products, half_step(): jnp.einsum('eic,eik->eck', left, right, preferred_element_type=jnp.float32)  13.3 us
    dot_general x1, matrix products, half_step(): jnp.einsum('eik,eck->eic', right, gram_block, preferred_element_type=jnp....  12.5 us

profile of v1, /device:TPU:6, one launch (start us, length us, event | category | flops | bytes accessed | tf_op | source)
XLA Modules:
  0.0 401.9 jit_solution(2808952853451094958)
XLA Ops:
  0.0 0.0 copy-start
  0.0 0.8 compare_and_fusion
  0.8 0.7 compare_select_fusion
  1.5 0.1 copy-done
  1.5 1.9 gather_fusion
  3.4 1.7 broadcast_select_fusion
  5.2 0.0 copy-start.2
  5.2 1.9 stack.2
  7.0 169.2 %all_to_all.5 = bf16[8,8,448,256]{3,2,1,0:T(8,128)(2,1)S(1)} all-to-all(bf16[8,8,448,256]{3,2,1,0:T(8,128)(2,1)S(1)} %stack.2), channel_id=1, replica_groups=mesh['fsdp'=16,'loop'=8] {'loop'}, dimensions={0} | all-to-all | bytes 29360128 | tf_op jit(solution)/shard_map/all_to_all | solution.py:15
  176.2 6.7 %copy.4 = bf16[8,8,56,8,256]{4,3,0,2,1:T(8,128)(2,1)} copy(bf16[8,8,56,8,256]{4,3,2,1,0:T(8,128)(2,1)S(1)} %bitcast.7) | data formatting | bytes 29360128 | tf_op jit(solution)/shard_map/reshape | solution.py:14
  182.9 0.0 copy-done.2
  182.9 13.3 %fusion.4 = f32[8,256,2048]{2,1,0:T(8,128)} fusion(bf16[8,448,256]{2,1,0:T(8,128)(2,1)S(1)} %broadcast_select_fusion, bf16[8,448,2048]{2,1,0:T(8,128)(2,1)} %bitcast.8), kind=kOutput, calls=%fused_computation.8 | convolution fusion | flops 3758096384 | bytes 33292288 | tf_op jit(solution)/shard_map/eic,eik->eck/dot_general | solution.py:24
  196.3 193.1 %all-reduce.1 = bf16[8,256,2048]{2,1,0:T(8,128)(2,1)} all-reduce(f32[8,256,2048]{2,1,0:T(8,128)} %fusion.4), channel_id=1, replica_groups=mesh['fsdp'=16,'loop'=8] {'fsdp'}, use_global_device_ids=true, to_apply=%region_0.1 | all-reduce | flops 4194304 | bytes 25165824 | tf_op jit(solution)/shard_map/psum | solution.py:25
  389.4 0.0 copy-start.1
  389.4 12.5 %multiply_convert_fusion = bf16[8,448,256]{2,1,0:T(8,128)(2,1)} fusion(bf16[8,448,256]{2,1,0:T(8,128)(2,1)} %copy-done.2, bf16[8,448,2048]{2,1,0:T(8,128)(2,1)} %bitcast.9, bf16[8,256,2048]{2,1,0:T(8,128)(2,1)} %all-reduce.1), kind=kOutput, calls=%fused_computation.3 | convolution fusion | flops 3763601408 | bytes 26738688 | tf_op jit(solution)/shard_map/eik,eck->eic/dot_general | solution.py:27
  401.9 0.0 copy-done.1
  (1 shorter events, 0.0 us)
Async XLA Ops:
  0.0 1.5 copy-start
  5.2 177.8 %copy-start.2 = (bf16[8,448,256]{2,1,0:T(8,128)(2,1)}, bf16[8,448,256]{2,1,0:T(8,128)(2,1)S(1)}, u32[]{:S(2)}) copy-start(bf16[8,448,256]{2,1,0:T(8,128)(2,1)S(1)} %broadcast_select_fusion) | copy-start | bytes 5505028
  389.4 12.5 %copy-start.1 = (bf16[8,448,256]{2,1,0:T(8,128)(2,1)S(1)}, bf16[8,448,256]{2,1,0:T(8,128)(2,1)}, u32[]{:S(2)}) copy-start(bf16[8,448,256]{2,1,0:T(8,128)(2,1)} %param.2) | copy-start | bytes 5505028
